TPU v7x, 32 devices: a whole 2x2x4 slice. The times are simulated.
32 devices in a mesh: groups: 2 (over y), seq: 4 (over z), head: 4 (over x, core).
Axes of the slice: x: 2, y: 2, z: 4, core: 2. Of those that a mesh axis runs over, the one named last changes fastest.
Arguments:
- doc_start: int32 [1024], P(('groups', 'seq')), parts along dimension 0, may hold values from 0 to 511, as said below
- q_gdn: bfloat16 [1024, 2048], P(('groups', 'seq'), 'head'), parts along dimension 0, may hold values from -6 to 6
- k_gdn: bfloat16 [1024, 2048], P(('groups', 'seq'), 'head'), parts along dimension 0, may hold values from -6 to 6
- v_gdn: bfloat16 [1024, 4096], P(('groups', 'seq'), 'head'), parts along dimension 0, may hold values from -6 to 6
- z_gdn: bfloat16 [1024, 4096], P(('groups', 'seq'), 'head'), parts along dimension 0, may hold values from -6 to 6
- beta_logit: float32 [32, 1024], P('head', ('groups', 'seq')), parts along dimension 1, may hold values from -8 to 3
- log_decay: float32 [32, 1024], P('head', ('groups', 'seq')), parts along dimension 1, may hold values from -1 to 0
- norm_weight: float32 [128], replicated, may hold values from 0.1 to 1.9
- q_attn: bfloat16 [1024, 4096], P(('groups', 'seq'), 'head'), parts along dimension 0, may hold values from -6 to 6
- k_attn: bfloat16 [1024, 512], P(('groups', 'seq')), parts along dimension 0, may hold values from -6 to 6
- v_attn: bfloat16 [1024, 512], P(('groups', 'seq')), parts along dimension 0, may hold values from -6 to 6
- gate_attn: bfloat16 [1024, 4096], P(('groups', 'seq'), 'head'), parts along dimension 0, may hold values from -6 to 6
Outputs:
- gdn_out: bfloat16 [1024, 4096], P(('groups', 'seq'), 'head'), parts along dimension 0
- attn_out: bfloat16 [1024, 4096], P(('groups', 'seq'), 'head'), parts along dimension 0
There are 2 independent parts, one for each index of `groups`. A program takes and returns all parts, laid end to end along the dimension named above; an argument that names none is the same for every part. Nothing has to cross between parts.
Inputs may be any that keep to these rules, and one draw needn't show every extreme that they name: Nondecreasing; doc_start[i] <= i, with equality exactly at the first token of each of the 3 documents; the first document starts at 0.
All inputs are finite; a program needn't handle non-finite values.
Results may differ from a plain program's by a relative error of at most 0.0095.
Values may be sent and summed in bfloat16 or wider, within the bound.
A program may use at most 128 MiB of HBM per device.

v0:
```python
import jax
import jax.numpy as jnp
from jax import lax
from jax.sharding import PartitionSpec as P

DK = 128
DV = 128
QH = 16
KVH = 2
HD_A = 256
BLOCK = 64


HIGH = lax.Precision.HIGHEST


def shifted(shard, axis, by):
    length = lax.axis_size(axis)
    pairs = [(i, i + by) for i in range(length) if 0 <= i + by < length]
    return lax.ppermute(shard, axis, pairs)


def unit_rows(values):
    return values * lax.rsqrt(jnp.sum(values * values, axis=-1, keepdims=True) + 1e-06)


def blocked(values, count):
    length, heads, width = values.shape
    return values.reshape(count, length // count, heads, width).transpose(0, 2, 1, 3)


def block_terms(anchor, doc_block, query, keys, values, beta, log_gate):
    width = query.shape[1]
    running = jnp.cumsum(log_gate, axis=1)
    place = anchor + jnp.arange(width, dtype=jnp.int32)
    causal = place[None, :] <= place[:, None]
    same = causal & (doc_block[:, None] <= place[None, :])
    strict = same & (place[None, :] < place[:, None])
    spread = jnp.where(same[None], running[:, :, None] - running[:, None, :], 0.0)
    decay = jnp.where(same[None], jnp.exp(spread), 0.0)
    alive = (doc_block < anchor).astype(jnp.float32)
    entry = jnp.exp(running) * alive[None, :]
    gram = jnp.einsum("hik,hjk->hij", keys, keys, precision=HIGH)
    lower_part = jnp.where(strict[None], decay * gram, 0.0)
    system = jnp.eye(width, dtype=jnp.float32)[None] + beta[:, :, None] * lower_part
    right = jnp.concatenate([beta[:, :, None] * values, (beta * entry)[:, :, None] * keys], axis=2)
    solved = lax.linalg.triangular_solve(
        system, right, left_side=True, lower=True, unit_diagonal=True
    )
    fresh = solved[:, :, : values.shape[2]]
    erased = solved[:, :, values.shape[2] :]
    scores = jnp.einsum("hik,hjk->hij", query, keys, precision=HIGH) * decay
    local_out = jnp.einsum("hij,hjv->hiv", scores, fresh, precision=HIGH)
    reach = entry[:, :, None] * query - jnp.einsum("hij,hjk->hik", scores, erased, precision=HIGH)
    tail_keys = decay[:, -1, :, None] * keys
    identity = jnp.eye(keys.shape[2], dtype=jnp.float32)
    carry_map = entry[:, -1, None, None] * identity[None] - jnp.einsum(
        "hjk,hjl->hkl", erased, tail_keys, precision=HIGH
    )
    carry_add = jnp.einsum("hjv,hjk->hvk", fresh, tail_keys, precision=HIGH)
    return (local_out, reach, carry_map, carry_add)


def compose(earlier, later):
    joined_map = jnp.einsum("hkl,hlm->hkm", earlier[0], later[0], precision=HIGH)
    joined_add = jnp.einsum("hvl,hlm->hvm", earlier[1], later[0], precision=HIGH) + later[1]
    return (joined_map, joined_add)


def entering_state(device_map, device_add):

    def relay(turn, pair):
        incoming, state = pair
        incoming = shifted(state.astype(jnp.bfloat16), "seq", 1).astype(state.dtype)
        state = jnp.einsum("hvk,hkl->hvl", incoming, device_map, precision=HIGH) + device_add
        return (incoming, state)

    start_state, _ = lax.fori_loop(
        0, lax.axis_size("seq") - 1, relay, (jnp.zeros_like(device_add), device_add)
    )
    return start_state


def delta_layer(doc_start, q_gdn, k_gdn, v_gdn, z_gdn, beta_logit, log_decay, norm_weight, anchor):
    length = q_gdn.shape[0]
    key_heads = q_gdn.shape[1] // DK
    value_heads = v_gdn.shape[1] // DV
    repeat = value_heads // key_heads
    count = length // BLOCK
    query = jnp.repeat(
        unit_rows(q_gdn.astype(jnp.float32).reshape(length, key_heads, DK)), repeat, axis=1
    )
    keys = jnp.repeat(
        unit_rows(k_gdn.astype(jnp.float32).reshape(length, key_heads, DK)), repeat, axis=1
    )
    values = v_gdn.astype(jnp.float32).reshape(length, value_heads, DV)
    beta = jax.nn.sigmoid(beta_logit).reshape(value_heads, count, BLOCK).transpose(1, 0, 2)
    log_gate = log_decay.reshape(value_heads, count, BLOCK).transpose(1, 0, 2)
    docs = doc_start.reshape(count, BLOCK)
    anchors = anchor + BLOCK * jnp.arange(count, dtype=jnp.int32)
    identity = jnp.broadcast_to(jnp.eye(DK, dtype=jnp.float32), (value_heads, DK, DK))

    def sweep(totals, inputs):
        total_map, total_add = totals
        block_anchor, doc_block, q_block, k_block, v_block, b_block, g_block = inputs
        local_out, reach, carry_map, carry_add = block_terms(
            block_anchor, doc_block, q_block, k_block, v_block, b_block, g_block
        )
        joined = compose((total_map, total_add), (carry_map, carry_add))
        return (joined, (local_out, reach, total_map, total_add))

    start_totals = (identity, jnp.zeros((value_heads, DV, DK), jnp.float32))
    scanned = (
        anchors,
        docs,
        blocked(query, count),
        blocked(keys, count),
        blocked(values, count),
        beta,
        log_gate,
    )
    (device_map, device_add), (local_out, reach, prefix_map, prefix_add) = lax.scan(
        sweep, start_totals, scanned
    )
    start_state = entering_state(device_map, device_add)
    block_state = jnp.einsum("hvk,chkl->chvl", start_state, prefix_map, precision=HIGH) + prefix_add
    mixed = local_out + jnp.einsum("chik,chvk->chiv", reach, block_state, precision=HIGH)
    mixed = mixed.transpose(0, 2, 1, 3).reshape(length, value_heads, DV)
    gate = z_gdn.astype(jnp.float32).reshape(length, value_heads, DV)
    factor = lax.rsqrt(jnp.mean(mixed * mixed, axis=-1, keepdims=True) + 1e-06)
    normed = mixed * factor * norm_weight * jax.nn.silu(gate)
    return normed.reshape(length, value_heads * DV).astype(jnp.bfloat16)


def attend(doc_start, q_attn, k_attn, v_attn, gate_attn, anchor):
    length = q_attn.shape[0]
    local_heads = q_attn.shape[1] // HD_A
    group = QH // KVH
    shards_seen = lax.axis_size("seq") // 2 + 1
    window_size = shards_seen * length
    kv_head = lax.axis_index("head") * local_heads // group
    keys_own = lax.dynamic_slice_in_dim(k_attn, kv_head * HD_A, HD_A, 1)
    values_own = lax.dynamic_slice_in_dim(v_attn, kv_head * HD_A, HD_A, 1)
    query = q_attn.reshape(length, local_heads, HD_A)
    q_place = anchor + jnp.arange(length, dtype=jnp.int32)
    lower = jnp.maximum(doc_start, q_place - window_size + 1)
    lowest = jnp.min(lower)
    highest = anchor + length - 1
    factor = HD_A ** (-0.5)
    initial = (
        jnp.full((local_heads, length), -1e30, jnp.float32),
        jnp.zeros((local_heads, length), jnp.float32),
        jnp.zeros((local_heads, length, HD_A), jnp.float32),
    )
    key_piece = lax.all_gather(keys_own, "seq", axis=0, tiled=True)
    value_piece = lax.all_gather(values_own, "seq", axis=0, tiled=True)
    count = key_piece.shape[0]
    width = count
    while width > 1024 and width % 2 == 0:
        width = width // 2

    def one(index, inner):
        begin = index * width
        key_part = lax.dynamic_slice_in_dim(key_piece, begin, width, 0)
        value_part = lax.dynamic_slice_in_dim(value_piece, begin, width, 0)
        k_place = begin + jnp.arange(width, dtype=jnp.int32)

        def compute(state):
            peak, total, accum = state
            scores = (
                jnp.einsum("qhd,kd->hqk", query, key_part, preferred_element_type=jnp.float32)
                * factor
            )
            visible = (k_place[None, :] >= lower[:, None]) & (k_place[None, :] <= q_place[:, None])
            masked = jnp.where(visible[None], scores, -jnp.inf)
            new_peak = jnp.maximum(peak, jnp.max(masked, axis=-1))
            weights = jnp.exp(masked - new_peak[:, :, None])
            shrink = jnp.exp(peak - new_peak)
            total = total * shrink + jnp.sum(weights, axis=-1)
            update = jnp.einsum(
                "hqk,kd->hqd",
                weights.astype(jnp.bfloat16),
                value_part,
                preferred_element_type=jnp.float32,
            )
            accum = accum * shrink[:, :, None] + update
            return (new_peak, total, accum)

        def unchanged(state):
            return state

        busy = (begin <= highest) & (begin + width - 1 >= lowest)
        return lax.cond(busy, compute, unchanged, inner)

    peak, total, accum = lax.fori_loop(0, count // width, one, initial)
    mixed = (accum / total[:, :, None]).transpose(1, 0, 2).reshape(length, local_heads * HD_A)
    return (mixed * jax.nn.sigmoid(gate_attn.astype(jnp.float32))).astype(jnp.bfloat16)


def shards(
    doc_start,
    q_gdn,
    k_gdn,
    v_gdn,
    z_gdn,
    beta_logit,
    log_decay,
    norm_weight,
    q_attn,
    k_attn,
    v_attn,
    gate_attn,
):
    anchor = lax.axis_index("seq") * q_gdn.shape[0]
    gdn_out = delta_layer(
        doc_start, q_gdn, k_gdn, v_gdn, z_gdn, beta_logit, log_decay, norm_weight, anchor
    )
    attn_out = attend(doc_start, q_attn, k_attn, v_attn, gate_attn, anchor)
    return (gdn_out, attn_out)


def solution(mesh):
    return jax.shard_map(
        shards,
        mesh=mesh,
        in_specs=(
            P(("groups", "seq")),
            P(("groups", "seq"), "head"),
            P(("groups", "seq"), "head"),
            P(("groups", "seq"), "head"),
            P(("groups", "seq"), "head"),
            P("head", ("groups", "seq")),
            P("head", ("groups", "seq")),
            P(),
            P(("groups", "seq"), "head"),
            P(("groups", "seq"), None),
            P(("groups", "seq"), None),
            P(("groups", "seq"), "head"),
        ),
        out_specs=(P(("groups", "seq"), "head"), P(("groups", "seq"), "head")),
        check_vma=False,
    )
```

profile of v0, /device:TPU:26, one launch (start us, length us, event | category | flops | bytes accessed | tf_op | source)
XLA Modules:
  0.0 187.4 jit_solution(7092509554987152704)
XLA Ops:
  7.8 105.6 %while.13 = (s32[]{:T(128)}, f32[8,128,128]{1,2,0:T(8,128)S(1)}, f32[8,128,128]{1,2,0:T(8,128)S(1)}, f32[2,8,64,128]{3,2,1,0:T(8,128)}, f32[2,8,64,128]{3,2,1,0:...) while((s32[]{:T(128)}, f32[8,128,128]{1,2,0:T(8,128)S(1)}, ...), condition=%wide.region_4.5_spmd.clone, body=%wide.region_2.4_spmd.clone.sunk | while | flops 907780864 | bytes 40192524 | solution.py:122
  10.1 39.3 %custom-call.11 = f32[8,1,64,64]{2,3,1,0:T(8,128)S(1)} custom-call(f32[8,1,64,64]{3,2,1,0:T(8,128)S(1)} %fusion.124), custom_call_target="InvertDiagBlocksLowerTriangular" | custom-call | tf_op jit(solution)/shard_map/while/body/eval_jaxpr/triangular_solve | solution.py:47
  52.4 1.1 convolution_subtract_fusion.3
  55.2 1.1 convolution_add_fusion.7
  56.3 1.0 convolution_bitcast_fusion.6
  62.9 39.3 %custom-call.11 = f32[8,1,64,64]{2,3,1,0:T(8,128)S(1)} custom-call(f32[8,1,64,64]{3,2,1,0:T(8,128)S(1)} %fusion.124), custom_call_target="InvertDiagBlocksLowerTriangular" | custom-call | tf_op jit(solution)/shard_map/while/body/eval_jaxpr/triangular_solve | solution.py:47
  105.2 1.1 convolution_subtract_fusion.3
  108.0 1.1 convolution_add_fusion.7
  109.1 1.0 convolution_bitcast_fusion.6
  114.6 33.9 %while.12 = (s32[]{:T(128)}, f32[8,128,128]{2,1,0:T(8,128)}, bf16[8,128,128]{2,1,0:T(8,128)(2,1)}, f32[8,128,128]{2,1,0:T(8,128)S(1)}, f32[8,128,128]{2,1,0:T(8,128)S(1)}, /*index=5*/s32[]{:T(128)}) while((s32[]{:T(128)}, f32[8,128,128]{2,1,0:T(8,128)}, bf16[8,128,128]{2,1,0:T(8,128)(2,1)}, f32[8,128,128]{2,1,0:T(8,128)S(1)}, ...), condition=%wide.region_6.7_spmd, body=%wide.region_5.6_spmd.sunk | while | flops 201719808 | bytes 3407981 | solution.py:78
  114.6 1.4 collective-permute-start
  116.1 8.9 %collective-permute-done = bf16[8,128,128]{2,1,0:T(8,128)(2,1)S(1)} collective-permute-done((bf16[8,128,128]{2,1,0:T(8,128)(2,1)}, bf16[8,128,128]{2,1,0:T(8,128)(2,1)S(1)}, u32[]{:S(2)}, u32[]{:S(2)}) %collective-permute-start) | collective-permute-done | bytes 262176 | tf_op jit(solution)/shard_map/while/body/eval_jaxpr/ppermute | solution.py:20
  125.8 1.1 convolution_add_fusion.6
  126.9 1.3 collective-permute-start
  128.2 8.0 %collective-permute-done = bf16[8,128,128]{2,1,0:T(8,128)(2,1)S(1)} collective-permute-done((bf16[8,128,128]{2,1,0:T(8,128)(2,1)}, bf16[8,128,128]{2,1,0:T(8,128)(2,1)S(1)}, u32[]{:S(2)}, u32[]{:S(2)}) %collective-permute-start) | collective-permute-done | bytes 262176 | tf_op jit(solution)/shard_map/while/body/eval_jaxpr/ppermute | solution.py:20
  137.0 1.1 convolution_add_fusion.6
  138.1 1.3 collective-permute-start
  139.4 7.2 %collective-permute-done = bf16[8,128,128]{2,1,0:T(8,128)(2,1)S(1)} collective-permute-done((bf16[8,128,128]{2,1,0:T(8,128)(2,1)}, bf16[8,128,128]{2,1,0:T(8,128)(2,1)S(1)}, u32[]{:S(2)}, u32[]{:S(2)}) %collective-permute-start) | collective-permute-done | bytes 262176 | tf_op jit(solution)/shard_map/while/body/eval_jaxpr/ppermute | solution.py:20
  147.4 1.1 convolution_add_fusion.6
  148.5 2.2 %fusion.53 = f32[2,8,128,128]{2,3,1,0:T(8,128)S(1)} fusion(f32[2,8,128,128]{2,3,1,0:T(8,128)S(1)} %copy-done.6, f32[2,8,128,128]{2,3,1,0:T(8,128)S(1)} %copy-done.3, f32[8,128,128]{2,1,0:T(8,128)} %get-tuple-element.215), kind=kOutput, calls=%fused_computation.91 | convolution fusion | flops 402915328 | bytes 3670016 | tf_op jit(solution)/shard_map/hvk,chkl->chvl/dot_general | solution.py:126
  150.7 1.1 multiply_reduce_fusion
  154.2 14.1 %all_gather.6 = bf16[512,256]{1,0:T(8,128)(2,1)S(1)} all-gather(bf16[128,256]{1,0:T(8,128)(2,1)S(1)} %constant_dynamic-slice_fusion.5), channel_id=1, replica_groups=mesh['groups'=2,'seq'=4,'head'=4] {'seq'}, dimensions={0}, use_global_device_ids=true | all-gather | bytes 327680 | tf_op jit(solution)/shard_map/all_gather | solution.py:155
  168.3 14.4 %all_gather.7 = bf16[512,256]{1,0:T(8,128)(2,1)S(1)} all-gather(bf16[128,256]{1,0:T(8,128)(2,1)S(1)} %constant_dynamic-slice_fusion.4), channel_id=1, replica_groups=mesh['groups'=2,'seq'=4,'head'=4] {'seq'}, dimensions={0}, use_global_device_ids=true | all-gather | bytes 327680 | tf_op jit(solution)/shard_map/all_gather | solution.py:156
  184.2 1.2 conditional.1
  (167 shorter events, 36.9 us)
Async XLA Ops:
  0.6 153.5 %copy-start = (bf16[128,512]{1,0:T(8,128)(2,1)S(1)}, bf16[128,512]{1,0:T(8,128)(2,1)}, u32[]{:S(2)}) copy-start(bf16[128,512]{1,0:T(8,128)(2,1)} %param.27) | copy-start | bytes 393220
  53.5 1.2 copy-start.1
  53.5 1.5 copy-start.4
  55.2 2.2 %copy-start.2 = (f32[2,8,128,128]{2,3,1,0:T(8,128)}, f32[2,8,128,128]{2,3,1,0:T(8,128)S(1)}, u32[]{:S(2)}) copy-start(f32[2,8,128,128]{2,3,1,0:T(8,128)S(1)} %get-tuple-element.561) | copy-start | bytes 3145732 | tf_op jit(solution)/shard_map/while
  55.2 2.2 %copy-start.5 = (f32[2,8,128,128]{2,3,1,0:T(8,128)}, f32[2,8,128,128]{2,3,1,0:T(8,128)S(1)}, u32[]{:S(2)}) copy-start(f32[2,8,128,128]{2,3,1,0:T(8,128)S(1)} %get-tuple-element.562) | copy-start | bytes 3145732 | tf_op jit(solution)/shard_map/while
  57.3 1.0 copy-start.10
  58.4 1.0 copy-start.7
  58.8 1.0 copy-start.11
  106.3 1.2 copy-start.1
  106.3 1.5 copy-start.4
  108.0 2.2 %copy-start.2 = (f32[2,8,128,128]{2,3,1,0:T(8,128)}, f32[2,8,128,128]{2,3,1,0:T(8,128)S(1)}, u32[]{:S(2)}) copy-start(f32[2,8,128,128]{2,3,1,0:T(8,128)S(1)} %get-tuple-element.561) | copy-start | bytes 3145732 | tf_op jit(solution)/shard_map/while
  108.0 2.2 %copy-start.5 = (f32[2,8,128,128]{2,3,1,0:T(8,128)}, f32[2,8,128,128]{2,3,1,0:T(8,128)S(1)}, u32[]{:S(2)}) copy-start(f32[2,8,128,128]{2,3,1,0:T(8,128)S(1)} %get-tuple-element.562) | copy-start | bytes 3145732 | tf_op jit(solution)/shard_map/while
  110.2 1.0 copy-start.10
  111.2 1.0 copy-start.7
  111.6 1.0 copy-start.11
  114.6 33.9 %copy-start.3 = (f32[2,8,128,128]{2,3,1,0:T(8,128)S(1)}, f32[2,8,128,128]{2,3,1,0:T(8,128)}, u32[]{:S(2)}) copy-start(f32[2,8,128,128]{2,3,1,0:T(8,128)} %get-tuple-element.212) | copy-start | bytes 3145732
  114.6 33.9 %copy-start.6 = (f32[2,8,128,128]{2,3,1,0:T(8,128)S(1)}, f32[2,8,128,128]{2,3,1,0:T(8,128)}, u32[]{:S(2)}) copy-start(f32[2,8,128,128]{2,3,1,0:T(8,128)} %get-tuple-element.216) | copy-start | bytes 3145732
  114.6 10.3 %collective-permute-start = (bf16[8,128,128]{2,1,0:T(8,128)(2,1)}, bf16[8,128,128]{2,1,0:T(8,128)(2,1)S(1)}, u32[]{:S(2)}, u32[]{:S(2)}) collective-permute-start(bf16[8,128,128]{2,1,0:T(8,128)(2,1)} %get-tuple-element.581), channel_id=1, source_target_pairs={{0,4},{4,8},{8,12},{1,5},{5,9},{9,13},{2,6},{6,10},{10,14},{3,7},{... | collective-permute-start | bytes 786440 | tf_op jit(solution)/shard_map/while/body/eval_jaxpr/ppermute | solution.py:20
  126.9 9.3 %collective-permute-start = (bf16[8,128,128]{2,1,0:T(8,128)(2,1)}, bf16[8,128,128]{2,1,0:T(8,128)(2,1)S(1)}, u32[]{:S(2)}, u32[]{:S(2)}) collective-permute-start(bf16[8,128,128]{2,1,0:T(8,128)(2,1)} %get-tuple-element.581), channel_id=1, source_target_pairs={{0,4},{4,8},{8,12},{1,5},{5,9},{9,13},{2,6},{6,10},{10,14},{3,7},{... | collective-permute-start | bytes 786440 | tf_op jit(solution)/shard_map/while/body/eval_jaxpr/ppermute | solution.py:20
  138.1 8.5 %collective-permute-start = (bf16[8,128,128]{2,1,0:T(8,128)(2,1)}, bf16[8,128,128]{2,1,0:T(8,128)(2,1)S(1)}, u32[]{:S(2)}, u32[]{:S(2)}) collective-permute-start(bf16[8,128,128]{2,1,0:T(8,128)(2,1)} %get-tuple-element.581), channel_id=1, source_target_pairs={{0,4},{4,8},{8,12},{1,5},{5,9},{9,13},{2,6},{6,10},{10,14},{3,7},{... | collective-permute-start | bytes 786440 | tf_op jit(solution)/shard_map/while/body/eval_jaxpr/ppermute | solution.py:20
  148.5 2.2 %copy-start.9 = (f32[2,8,64,128]{3,2,1,0:T(8,128)S(1)}, f32[2,8,64,128]{3,2,1,0:T(8,128)}, u32[]{:S(2)}) copy-start(f32[2,8,64,128]{3,2,1,0:T(8,128)} %get-tuple-element.210) | copy-start | bytes 1572868
  148.5 2.2 %copy-start.12 = (f32[2,8,64,128]{3,2,1,0:T(8,128)S(1)}, f32[2,8,64,128]{3,2,1,0:T(8,128)}, u32[]{:S(2)}) copy-start(f32[2,8,64,128]{3,2,1,0:T(8,128)} %get-tuple-element.211) | copy-start | bytes 1572868
  152.2 1.0 copy-start.14
  154.2 14.1 %copy-start.17 = (bf16[128,512]{1,0:T(8,128)(2,1)S(1)}, bf16[128,512]{1,0:T(8,128)(2,1)}, u32[]{:S(2)}) copy-start(bf16[128,512]{1,0:T(8,128)(2,1)} %param.28) | copy-start | bytes 393220
  (10 other events, 8.1 us)
where the time goes:
time: 190 us; the launch traced here: 187 us
  other arithmetic  90.3 us (48%)
  blocking collectives  28.4 us (15%)
  waiting for transfers between devices  24 us (13%)
  matrix products  21.2 us (11%)
  local copies, waits for them, and re-layouts  17.3 us (9%)
  starting transfers between devices  3.98 us (2%)
    another operation x6, other arithmetic, block_terms(): lax.linalg.triangular_solve(system, right, left_side=True, lower=True, un...  78.8 us
    ppermute x3, waiting for transfers between devices, shifted(): return lax.ppermute(shard, axis, pairs)  24 us
    all_gather x1, blocking collectives, attend(): value_piece = lax.all_gather(values_own, 'seq', axis=0, tiled=True)  14.4 us
    all_gather x1, blocking collectives, attend(): key_piece = lax.all_gather(keys_own, 'seq', axis=0, tiled=True)  14.1 us
    unnamed x31, local copies, waits for them, and re-layouts  5.57 us
    while x34, local copies, waits for them, and re-layouts  4.79 us
    ppermute x3, starting transfers between devices, shifted(): return lax.ppermute(shard, axis, pairs)  3.98 us
  transfers between devices with their start and end apart: 3, of which 3 were waited for; matrix products, arithmetic and copies ran while one was open for 0% of the time, Pallas kernels for 0%

commit v1 on v0

v1 whole, which is shorter than its diff:
```python
import functools

import jax
import jax.numpy as jnp
from jax import lax
from jax.experimental import pallas as pl
from jax.experimental.pallas import tpu as pltpu
from jax.sharding import PartitionSpec as P

DK = 128
DV = 128
QH = 16
KVH = 2
HD_A = 256
NEG = -1e30

MESH = pl.DeviceIdType.MESH
BF = jnp.bfloat16
F32 = jnp.float32


def dot(a, b):
    return jnp.dot(a.astype(BF), b.astype(BF), preferred_element_type=F32)


def dot_t(a, b):
    return lax.dot_general(a, b, (((1,), (1,)), ((), ())), preferred_element_type=F32)


def unit_rows(values):
    return values * lax.rsqrt(jnp.sum(values * values, axis=-1, keepdims=True) + 1e-06)


def running_sum(rows, lane):
    width = rows.shape[1]
    step = 1
    while step < width:
        rows = rows + jnp.where(lane >= step, pltpu.roll(rows, step, 1), 0.0)
        step *= 2
    return rows


def kernel(
    devices,
    seen,
    doc_ref,
    q_ref,
    k_ref,
    v_ref,
    z_ref,
    beta_ref,
    gate_ref,
    norm_ref,
    qa_ref,
    ka_ref,
    va_ref,
    ga_ref,
    gdn_ref,
    attn_ref,
    keys_buf,
    vals_buf,
    state_in,
    state_out,
    local_buf,
    reach_buf,
    map_buf,
    add_buf,
    kv_send,
    kv_recv,
    st_send,
    st_recv,
):
    me = lax.axis_index("seq")
    length = q_ref.shape[0]
    heads = v_ref.shape[1] // DV
    key_heads = q_ref.shape[1] // DK
    repeat = heads // key_heads
    attn_heads = qa_ref.shape[1] // HD_A
    kv = lax.axis_index("head") * attn_heads // (QH // KVH)
    columns = pl.ds(pl.multiple_of(kv * HD_A, HD_A), HD_A)
    anchor = me * length

    barrier = pltpu.get_barrier_semaphore()
    for r in range(1, seen + 1):
        @pl.when(me + r < devices)
        def _():
            pl.semaphore_signal(barrier, inc=1, device_id={"seq": me + r}, device_id_type=MESH)

        @pl.when(me - r >= 0)
        def _():
            pl.semaphore_signal(barrier, inc=1, device_id={"seq": me - r}, device_id_type=MESH)

    pl.semaphore_wait(barrier, jnp.minimum(me, seen) + jnp.minimum(devices - 1 - me, seen))

    def kv_copies(r):
        rows = pl.ds((seen - r) * length, length)
        return [
            pltpu.make_async_remote_copy(
                src_ref=src.at[:, columns],
                dst_ref=dst.at[rows, :],
                send_sem=kv_send.at[r - 1, which],
                recv_sem=kv_recv.at[r - 1, which],
                device_id={"seq": me + r},
                device_id_type=MESH,
            )
            for which, (src, dst) in enumerate(((ka_ref, keys_buf), (va_ref, vals_buf)))
        ]

    def state_copy(h):
        return pltpu.make_async_remote_copy(
            src_ref=state_out.at[h],
            dst_ref=state_in.at[h],
            send_sem=st_send.at[h],
            recv_sem=st_recv.at[h],
            device_id={"seq": me + 1},
            device_id_type=MESH,
        )

    for r in range(1, seen + 1):
        @pl.when(me + r < devices)
        def _():
            for copy in kv_copies(r):
                copy.start()

    row = lax.broadcasted_iota(jnp.int32, (length, length), 0)
    col = lax.broadcasted_iota(jnp.int32, (length, length), 1)
    lane = lax.broadcasted_iota(jnp.int32, (heads, length), 1)
    docs = doc_ref[...]
    run = running_sum(gate_ref[...], lane)
    beta = jax.nn.sigmoid(beta_ref[...])
    alive = docs < anchor
    entry = jnp.where(alive, jnp.exp(run), 0.0)
    last_run = run[:, length - 1 :]
    doc_last = docs[:, length - 1 :]
    tail = jnp.where(doc_last <= anchor + lane, jnp.exp(last_run - run), 0.0)
    entry_last = entry[:, length - 1 :]
    doc_rows = jnp.broadcast_to((docs - anchor).astype(F32), (heads, length))
    stacked = jnp.concatenate([run, beta, entry, doc_rows], axis=0)
    stacked = jnp.concatenate(
        [stacked, jnp.zeros((length - stacked.shape[0], length), F32)], axis=0
    )
    cols = stacked.T

    def column(kind, h):
        at = kind * heads + h
        return cols[:, at : at + 1]

    doc_col = column(3, 0).astype(jnp.int32)
    same = (col <= row) & (doc_col <= col)
    strict = same & (col < row)
    eye = jnp.where(row == col, 1.0, 0.0).astype(F32)
    differ = row ^ col
    levels = 0
    while (1 << levels) < length:
        levels += 1

    def local(group):
        qn, kn, knt, gram, cross = {}, {}, {}, {}, {}
        for g in sorted({h // repeat for h in group}):
            at = slice(g * DK, (g + 1) * DK)
            qn[g] = unit_rows(q_ref[:, at].astype(F32))
            kn[g] = unit_rows(k_ref[:, at].astype(F32))
            knt[g] = kn[g].T
            both = dot(jnp.concatenate([kn[g], qn[g]], axis=0), knt[g])
            gram[g], cross[g] = both[:length], both[length:]
        lower, scores, inverse = {}, {}, {}
        for h in group:
            g = h // repeat
            spread = jnp.where(same, column(0, h) - run[h : h + 1, :], 0.0)
            decay = jnp.where(same, jnp.exp(spread), 0.0)
            lower[h] = jnp.where(strict, column(1, h) * decay * gram[g], 0.0)
            scores[h] = (cross[g] * decay).astype(BF)
            inverse[h] = eye - jnp.where(differ == 1, lower[h], 0.0)
        for level in range(1, levels):
            mask = (differ >> level) == 1
            half = {}
            for h in group:
                part = jnp.where(mask, lower[h], 0.0)
                half[h] = dot(inverse[h], part)
            for h in group:
                inverse[h] = inverse[h] - dot(half[h], inverse[h])
        for h in group:
            g = h // repeat
            values = v_ref[:, h * DV : (h + 1) * DV].astype(F32)
            b = column(1, h)
            right = jnp.concatenate([b * values, (b * column(2, h)) * kn[g]], axis=1)
            solved = dot(inverse[h], right)
            tail_keys = knt[g] * tail[h : h + 1, :]
            left = jnp.concatenate([scores[h], tail_keys.astype(BF)], axis=0)
            made = dot(left, solved)
            local_buf[h] = made[:length, :DV]
            reach_buf[h] = (column(2, h) * qn[g] - made[:length, DV:]).astype(BF)
            map_buf[h] = (entry_last[h : h + 1, :] * eye - made[length:, DV:]).astype(BF)
            add_buf[h] = made[length:, :DV]

            @pl.when(me == 0)
            def _():
                state_in[h] = jnp.zeros(state_in.shape[1:], BF)
                state_out[h] = add_buf[h].astype(BF)
                if devices > 1:
                    state_copy(h).start()

    per_group = 4
    for first in range(0, heads, per_group):
        local(list(range(first, min(first + per_group, heads))))

    for h in range(heads):
        @pl.when(me > 0)
        def _():
            state_copy(h).wait_recv()

            @pl.when(me < devices - 1)
            def _():
                fresh = add_buf[h] + dot(map_buf[h], state_in[h])
                state_out[h] = fresh.astype(BF)
                state_copy(h).start()

    own = pl.ds(seen * length, length)
    keys_buf[own, :] = ka_ref[:, columns]
    vals_buf[own, :] = va_ref[:, columns]
    for r in range(1, seen + 1):
        @pl.when(me - r >= 0)
        def _():
            for copy in kv_copies(r):
                copy.wait_recv()

        @pl.when(me - r < 0)
        def _():
            rows = pl.ds((seen - r) * length, length)
            keys_buf[rows, :] = jnp.zeros((length, HD_A), BF)
            vals_buf[rows, :] = jnp.zeros((length, HD_A), BF)

    span = (seen + 1) * length
    window = (devices // 2 + 1) * length
    q_at = lax.broadcasted_iota(jnp.int32, (length, span), 0)
    k_at = lax.broadcasted_iota(jnp.int32, (length, span), 1) - seen * length
    floor = jnp.maximum(doc_col, q_at - window + 1)
    visible = (k_at >= floor) & (k_at <= q_at)
    factor = HD_A ** (-0.5)
    for a in range(attn_heads):
        at = slice(a * HD_A, (a + 1) * HD_A)
        raw = dot_t(qa_ref[:, at], keys_buf[...]) * factor
        masked = jnp.where(visible, raw, NEG)
        peak = jnp.max(masked, axis=-1, keepdims=True)
        weights = jnp.exp(masked - peak)
        total = jnp.sum(weights, axis=-1, keepdims=True)
        mixed = jnp.dot(weights.astype(BF), vals_buf[...], preferred_element_type=F32)
        gated = mixed / total * jax.nn.sigmoid(ga_ref[:, at].astype(F32))
        attn_ref[:, at] = gated.astype(BF)

    gain = norm_ref[...]
    for h in range(heads):
        at = slice(h * DV, (h + 1) * DV)
        mixed = local_buf[h] + dot(reach_buf[h], state_in[h])
        spread = lax.rsqrt(jnp.mean(mixed * mixed, axis=-1, keepdims=True) + 1e-06)
        gate = z_ref[:, at].astype(F32)
        gdn_ref[:, at] = (mixed * spread * gain * jax.nn.silu(gate)).astype(BF)

    for r in range(1, seen + 1):
        @pl.when(me + r < devices)
        def _():
            for copy in kv_copies(r):
                copy.wait_send()

    if devices > 1:
        @pl.when(me < devices - 1)
        def _():
            for h in range(heads):
                state_copy(h).wait_send()


def shards(
    devices,
    doc_start,
    q_gdn,
    k_gdn,
    v_gdn,
    z_gdn,
    beta_logit,
    log_decay,
    norm_weight,
    q_attn,
    k_attn,
    v_attn,
    gate_attn,
):
    length = q_gdn.shape[0]
    heads = v_gdn.shape[1] // DV
    seen = min(devices // 2 + 1, devices - 1)
    span = (seen + 1) * length
    whole = pl.BlockSpec(memory_space=pltpu.VMEM)
    return pl.pallas_call(
        functools.partial(kernel, devices, seen),
        out_shape=(
            jax.ShapeDtypeStruct(v_gdn.shape, BF),
            jax.ShapeDtypeStruct(q_attn.shape, BF),
        ),
        in_specs=[whole] * 12,
        out_specs=(whole, whole),
        scratch_shapes=[
            pltpu.VMEM((span, HD_A), BF),
            pltpu.VMEM((span, HD_A), BF),
            pltpu.VMEM((heads, DK, DV), BF),
            pltpu.VMEM((heads, DK, DV), BF),
            pltpu.VMEM((heads, length, DV), F32),
            pltpu.VMEM((heads, length, DK), BF),
            pltpu.VMEM((heads, DK, DK), BF),
            pltpu.VMEM((heads, DK, DV), F32),
            pltpu.SemaphoreType.DMA((seen, 2)),
            pltpu.SemaphoreType.DMA((seen, 2)),
            pltpu.SemaphoreType.DMA((heads,)),
            pltpu.SemaphoreType.DMA((heads,)),
        ],
        compiler_params=pltpu.CompilerParams(collective_id=0, has_side_effects=True),
    )(
        doc_start.reshape(1, length),
        q_gdn,
        k_gdn,
        v_gdn,
        z_gdn,
        beta_logit,
        log_decay,
        norm_weight.reshape(1, DV),
        q_attn,
        k_attn,
        v_attn,
        gate_attn,
    )


def solution(mesh):
    return jax.shard_map(
        functools.partial(shards, mesh.shape["seq"]),
        mesh=mesh,
        in_specs=(
            P(("groups", "seq")),
            P(("groups", "seq"), "head"),
            P(("groups", "seq"), "head"),
            P(("groups", "seq"), "head"),
            P(("groups", "seq"), "head"),
            P("head", ("groups", "seq")),
            P("head", ("groups", "seq")),
            P(),
            P(("groups", "seq"), "head"),
            P(("groups", "seq"), None),
            P(("groups", "seq"), None),
            P(("groups", "seq"), "head"),
        ),
        out_specs=(P(("groups", "seq"), "head"), P(("groups", "seq"), "head")),
        check_vma=False,
    )
```

time: 190 us -> 31 us (0.16); the launches traced: 187 us -> 30.8 us
  other arithmetic: 90.3 us -> 0 us
  blocking collectives: 28.4 us -> 0 us
  Pallas kernels: 0 us -> 27.7 us
  waiting for transfers between devices: 24 us -> 0 us
  matrix products: 21.2 us -> 0 us
  local copies, waits for them, and re-layouts: 17.3 us -> 2.42 us
  starting transfers between devices: 3.98 us -> 0 us
    another operation x13 -> x0, other arithmetic: 79.3 us -> none  [the longest x6 78.8 us: block_terms(): lax.linalg.triangular_solve(system, right, left_side=True, lower=True, un...]
    all_gather x2 -> x0, blocking collectives: 28.4 us -> none  [the longest x1 14.4 us: attend(): value_piece = lax.all_gather(values_own, 'seq', axis=0, tiled=True)]
    pallas_call x0 -> x1, Pallas kernels: none -> 27.7 us  [shards(): pl.pallas_call(functools.partial(kernel, devices, seen), out_shape=(jax.S...]
    ppermute x3 -> x0, waiting for transfers between devices: 24 us -> none  [shifted(): return lax.ppermute(shard, axis, pairs)]
    dot_general x23 -> x0, matrix products: 19.9 us -> none  [the longest x3 3.32 us: relay(): jnp.einsum('hvk,hkl->hvl', incoming, device_map, precision=HIGH)]
    while x36 -> x0, local copies, waits for them, and re-layouts: 5.18 us -> none
    convert_element_type x8 -> x0, other arithmetic: 4.37 us -> none  [the longest x3 2.51 us: relay(): incoming = shifted(state.astype(jnp.bfloat16), 'seq', 1).astype(state.dtype)]
    ppermute x3 -> x0, starting transfers between devices: 3.98 us -> none  [shifted(): return lax.ppermute(shard, axis, pairs)]
  transfers between devices with their start and end apart: 3 -> 0, of which waited for: 3 -> 0; matrix products, arithmetic and copies ran while one was open for 0% -> 0% of each run, Pallas kernels for 0% -> 0%
where the time goes in v1:
time: 31 us; the launch traced here: 30.8 us
  Pallas kernels  27.7 us (89%)
  local copies, waits for them, and re-layouts  2.42 us (8%)
  between operations  0.65 us (2%)
    pallas_call x1, Pallas kernels, shards(): pl.pallas_call(functools.partial(kernel, devices, seen), out_shape=(jax.S...  27.7 us
    unnamed x4, local copies, waits for them, and re-layouts  2.42 us

profile of v1, /device:TPU:26, one launch (start us, length us, event | category | flops | bytes accessed | tf_op | source)
XLA Modules:
  0.0 30.8 jit_solution(129158671547361681)
XLA Ops:
  0.6 27.7 %shard_map.131 = (bf16[128,1024]{1,0:T(8,128)(2,1)}, bf16[128,1024]{1,0:T(8,128)(2,1)}) custom-call(s32[1,128]{1,0:T(1,128)} %bitcast.2, bf16[128,512]{1,0:T(8,128)(2,1)} %q_ref.1, bf16[128,512]{1,0:T(8,128)(2,1)} %k_ref.1, bf16[128,1024]{1,0:T(8,128)(2,1)} %v_ref.1, bf16[128,1024]{1,0:T(8,128)(2,1)} %z_ref.1, f32[8,128]{1,0:T(8,128)} %beta_ref.1, ...), custom_call_target="tpu_custom_call" | custom-call | tf_op jit(solution)/shard_map/pallas_call | solution.py:292
  28.4 0.0 copy-start
  28.4 1.7 %copy.16 = bf16[128,1024]{1,0:T(8,128)(2,1)} copy(bf16[128,1024]{1,0:T(8,128)(2,1)} %get-tuple-element.4) | data formatting | bytes 524288
  30.1 0.0 copy-done
  30.1 0.7 %copy.17 = bf16[128,1024]{1,0:T(8,128)(2,1)} copy(bf16[128,1024]{1,0:T(8,128)(2,1)S(1)} %copy-done) | data formatting | bytes 524288
Async XLA Ops:
  28.4 1.7 %copy-start = (bf16[128,1024]{1,0:T(8,128)(2,1)S(1)}, bf16[128,1024]{1,0:T(8,128)(2,1)}, u32[]{:S(2)}) copy-start(bf16[128,1024]{1,0:T(8,128)(2,1)} %get-tuple-element.5) | copy-start | bytes 786436

commit v2 on v1

--- a/solution.py
+++ b/solution.py
@@ -25,10 +25,6 @@
 
 def dot_t(a, b):
     return lax.dot_general(a, b, (((1,), (1,)), ((), ())), preferred_element_type=F32)
-
-
-def unit_rows(values):
-    return values * lax.rsqrt(jnp.sum(values * values, axis=-1, keepdims=True) + 1e-06)
 
 
 def running_sum(rows, lane):
@@ -65,6 +61,9 @@
     reach_buf,
     map_buf,
     add_buf,
+    qn_buf,
+    score_buf,
+    solved_buf,
     kv_send,
     kv_recv,
     st_send,
@@ -154,59 +153,73 @@
     while (1 << levels) < length:
         levels += 1
 
-    def local(group):
-        qn, kn, knt, gram, cross = {}, {}, {}, {}, {}
+    ones = jnp.ones((DK, DK), BF)
+
+    def square_sum(values):
+        squares = values * values
+        high = squares.astype(BF)
+        low = (squares - high.astype(F32)).astype(BF)
+        return jnp.dot(high, ones, preferred_element_type=F32) + jnp.dot(
+            low, ones, preferred_element_type=F32
+        )
+
+    def unit_rows(values):
+        return values * lax.rsqrt(square_sum(values) + 1e-06)
+
+    def state_part(group):
+        kn, knt, gram, cross = {}, {}, {}, {}
         for g in sorted({h // repeat for h in group}):
             at = slice(g * DK, (g + 1) * DK)
-            qn[g] = unit_rows(q_ref[:, at].astype(F32))
-            kn[g] = unit_rows(k_ref[:, at].astype(F32))
+            qn = unit_rows(q_ref[:, at].astype(F32)).astype(BF)
+            kn[g] = unit_rows(k_ref[:, at].astype(F32)).astype(BF)
+            qn_buf[g] = qn
             knt[g] = kn[g].T
-            both = dot(jnp.concatenate([kn[g], qn[g]], axis=0), knt[g])
+            both = dot(jnp.concatenate([kn[g], qn], axis=0), knt[g])
             gram[g], cross[g] = both[:length], both[length:]
-        lower, scores, inverse = {}, {}, {}
+        inverse = {}
         for h in group:
             g = h // repeat
             spread = jnp.where(same, column(0, h) - run[h : h + 1, :], 0.0)
             decay = jnp.where(same, jnp.exp(spread), 0.0)
-            lower[h] = jnp.where(strict, column(1, h) * decay * gram[g], 0.0)
-            scores[h] = (cross[g] * decay).astype(BF)
-            inverse[h] = eye - jnp.where(differ == 1, lower[h], 0.0)
-        for level in range(1, levels):
+            lower = jnp.where(strict, column(1, h) * decay * gram[g], 0.0)
+            score_buf[h] = (cross[g] * decay).astype(BF)
+            inverse[h] = eye + lower
+        for level in range(levels):
             mask = (differ >> level) == 1
-            half = {}
             for h in group:
-                part = jnp.where(mask, lower[h], 0.0)
-                half[h] = dot(inverse[h], part)
-            for h in group:
-                inverse[h] = inverse[h] - dot(half[h], inverse[h])
+                whole = inverse[h]
+                part = jnp.where(mask, whole, 0.0)
+                inverse[h] = jnp.where(mask, 0.0, whole) - dot(part, whole)
+        solved = {}
         for h in group:
             g = h // repeat
             values = v_ref[:, h * DV : (h + 1) * DV].astype(F32)
             b = column(1, h)
-            right = jnp.concatenate([b * values, (b * column(2, h)) * kn[g]], axis=1)
-            solved = dot(inverse[h], right)
-            tail_keys = knt[g] * tail[h : h + 1, :]
-            left = jnp.concatenate([scores[h], tail_keys.astype(BF)], axis=0)
-            made = dot(left, solved)
-            local_buf[h] = made[:length, :DV]
-            reach_buf[h] = (column(2, h) * qn[g] - made[:length, DV:]).astype(BF)
-            map_buf[h] = (entry_last[h : h + 1, :] * eye - made[length:, DV:]).astype(BF)
-            add_buf[h] = made[length:, :DV]
-
+            right = jnp.concatenate(
+                [b * values, (b * column(2, h)) * kn[g].astype(F32)], axis=1
+            )
+            solved[h] = dot(inverse[h], right).astype(BF)
+            solved_buf[h] = solved[h]
+        for h in group:
+            g = h // repeat
+            tail_keys = (knt[g].astype(F32) * tail[h : h + 1, :]).astype(BF)
+            made = dot(tail_keys, solved[h])
+            map_buf[h] = (entry_last[h : h + 1, :] * eye - made[:, DV:]).astype(BF)
+            add_buf[h] = made[:, :DV]
+            state_out[h] = made[:, :DV].astype(BF)
+
+        if devices > 1:
             @pl.when(me == 0)
             def _():
-                state_in[h] = jnp.zeros(state_in.shape[1:], BF)
-                state_out[h] = add_buf[h].astype(BF)
-                if devices > 1:
+                for h in group:
                     state_copy(h).start()
 
     per_group = 4
     for first in range(0, heads, per_group):
-        local(list(range(first, min(first + per_group, heads))))
-
-    for h in range(heads):
-        @pl.when(me > 0)
-        def _():
+        state_part(list(range(first, min(first + per_group, heads))))
+
+    def relay():
+        for h in range(heads):
             state_copy(h).wait_recv()
 
             @pl.when(me < devices - 1)
@@ -215,9 +228,28 @@
                 state_out[h] = fresh.astype(BF)
                 state_copy(h).start()
 
+    @pl.when(me == 0)
+    def _():
+        state_in[...] = jnp.zeros(state_in.shape, BF)
+
+    @pl.when(me == 1)
+    def _():
+        relay()
+
     own = pl.ds(seen * length, length)
     keys_buf[own, :] = ka_ref[:, columns]
     vals_buf[own, :] = va_ref[:, columns]
+    for h in range(heads):
+        made = dot(score_buf[h], solved_buf[h])
+        local_buf[h] = made[:, :DV]
+        through = column(2, h) * qn_buf[h // repeat].astype(F32)
+        reach_buf[h] = (through - made[:, DV:]).astype(BF)
+
+    if devices > 2:
+        @pl.when(me == 2)
+        def _():
+            relay()
+
     for r in range(1, seen + 1):
         @pl.when(me - r >= 0)
         def _():
@@ -248,11 +280,16 @@
         gated = mixed / total * jax.nn.sigmoid(ga_ref[:, at].astype(F32))
         attn_ref[:, at] = gated.astype(BF)
 
+    if devices > 3:
+        @pl.when(me >= 3)
+        def _():
+            relay()
+
     gain = norm_ref[...]
     for h in range(heads):
         at = slice(h * DV, (h + 1) * DV)
         mixed = local_buf[h] + dot(reach_buf[h], state_in[h])
-        spread = lax.rsqrt(jnp.mean(mixed * mixed, axis=-1, keepdims=True) + 1e-06)
+        spread = lax.rsqrt(square_sum(mixed) * (1.0 / DV) + 1e-06)
         gate = z_ref[:, at].astype(F32)
         gdn_ref[:, at] = (mixed * spread * gain * jax.nn.silu(gate)).astype(BF)
 
@@ -306,6 +343,9 @@
             pltpu.VMEM((heads, length, DK), BF),
             pltpu.VMEM((heads, DK, DK), BF),
             pltpu.VMEM((heads, DK, DV), F32),
+            pltpu.VMEM((q_gdn.shape[1] // DK, length, DK), BF),
+            pltpu.VMEM((heads, length, length), BF),
+            pltpu.VMEM((heads, length, DV + DK), BF),
             pltpu.SemaphoreType.DMA((seen, 2)),
             pltpu.SemaphoreType.DMA((seen, 2)),
             pltpu.SemaphoreType.DMA((heads,)),

time: 31 us -> 30.2 us (0.974)
  Pallas kernels: 27.7 us -> 27 us
    pallas_call x1, Pallas kernels: 27.7 us -> 27 us  [shards(): pl.pallas_call(functools.partial(kernel, devices, seen), out_shape=(jax.S...]
where the time goes in v2:
time: 30.2 us; the launch traced here: 30 us
  Pallas kernels  27 us (89%)
  local copies, waits for them, and re-layouts  2.42 us (8%)
  between operations  0.65 us (2%)
    pallas_call x1, Pallas kernels, shards(): pl.pallas_call(functools.partial(kernel, devices, seen), out_shape=(jax.S...  27 us
    unnamed x4, local copies, waits for them, and re-layouts  2.42 us

profile of v2, /device:TPU:26, one launch (start us, length us, event | category | flops | bytes accessed | tf_op | source)
XLA Modules:
  0.0 30.0 jit_solution(5867793091689834321)
XLA Ops:
  0.6 27.0 %shard_map.131 = (bf16[128,1024]{1,0:T(8,128)(2,1)}, bf16[128,1024]{1,0:T(8,128)(2,1)}) custom-call(s32[1,128]{1,0:T(1,128)} %bitcast.2, bf16[128,512]{1,0:T(8,128)(2,1)} %q_ref.1, bf16[128,512]{1,0:T(8,128)(2,1)} %k_ref.1, bf16[128,1024]{1,0:T(8,128)(2,1)} %v_ref.1, bf16[128,1024]{1,0:T(8,128)(2,1)} %z_ref.1, f32[8,128]{1,0:T(8,128)} %beta_ref.1, ...), custom_call_target="tpu_custom_call" | custom-call | tf_op jit(solution)/shard_map/pallas_call | solution.py:329
  27.6 0.0 copy-start
  27.6 1.7 %copy.16 = bf16[128,1024]{1,0:T(8,128)(2,1)} copy(bf16[128,1024]{1,0:T(8,128)(2,1)} %get-tuple-element.4) | data formatting | bytes 524288
  29.3 0.0 copy-done
  29.3 0.7 %copy.17 = bf16[128,1024]{1,0:T(8,128)(2,1)} copy(bf16[128,1024]{1,0:T(8,128)(2,1)S(1)} %copy-done) | data formatting | bytes 524288
Async XLA Ops:
  27.6 1.7 %copy-start = (bf16[128,1024]{1,0:T(8,128)(2,1)S(1)}, bf16[128,1024]{1,0:T(8,128)(2,1)}, u32[]{:S(2)}) copy-start(bf16[128,1024]{1,0:T(8,128)(2,1)} %get-tuple-element.5) | copy-start | bytes 786436

commit v3 on v2

--- a/solution.py
+++ b/solution.py
@@ -53,8 +53,7 @@
     ga_ref,
     gdn_ref,
     attn_ref,
-    keys_buf,
-    vals_buf,
+    kv_buf,
     state_in,
     state_out,
     local_buf,
@@ -66,6 +65,8 @@
     solved_buf,
     kv_send,
     kv_recv,
+    ex_send,
+    ex_recv,
     st_send,
     st_recv,
 ):
@@ -79,31 +80,58 @@
     columns = pl.ds(pl.multiple_of(kv * HD_A, HD_A), HD_A)
     anchor = me * length
 
+    head = lax.axis_index("head")
+    part = head % 2
+    partner = head + 1 - 2 * part
+
     barrier = pltpu.get_barrier_semaphore()
-    for r in range(1, seen + 1):
-        @pl.when(me + r < devices)
-        def _():
-            pl.semaphore_signal(barrier, inc=1, device_id={"seq": me + r}, device_id_type=MESH)
-
-        @pl.when(me - r >= 0)
-        def _():
-            pl.semaphore_signal(barrier, inc=1, device_id={"seq": me - r}, device_id_type=MESH)
-
-    pl.semaphore_wait(barrier, jnp.minimum(me, seen) + jnp.minimum(devices - 1 - me, seen))
-
-    def kv_copies(r):
-        rows = pl.ds((seen - r) * length, length)
-        return [
-            pltpu.make_async_remote_copy(
-                src_ref=src.at[:, columns],
-                dst_ref=dst.at[rows, :],
-                send_sem=kv_send.at[r - 1, which],
-                recv_sem=kv_recv.at[r - 1, which],
-                device_id={"seq": me + r},
-                device_id_type=MESH,
-            )
-            for which, (src, dst) in enumerate(((ka_ref, keys_buf), (va_ref, vals_buf)))
-        ]
+    pl.semaphore_signal(barrier, inc=1, device_id={"head": partner}, device_id_type=MESH)
+
+    @pl.when(me < devices - 1)
+    def _():
+        pl.semaphore_signal(barrier, inc=1, device_id={"seq": me + 1}, device_id_type=MESH)
+
+    @pl.when(me > 0)
+    def _():
+        pl.semaphore_signal(barrier, inc=1, device_id={"seq": me - 1}, device_id_type=MESH)
+
+    pl.semaphore_wait(barrier, 1 + jnp.minimum(me, 1) + jnp.minimum(devices - 1 - me, 1))
+
+    def rows_of(r):
+        return pl.ds((seen - r) * length, length)
+
+    def hop(r, source):
+        return pltpu.make_async_remote_copy(
+            src_ref=source,
+            dst_ref=kv_buf.at[part, rows_of(r), :],
+            send_sem=kv_send.at[r - 1],
+            recv_sem=kv_recv.at[r - 1],
+            device_id={"seq": me + 1},
+            device_id_type=MESH,
+        )
+
+    def exchange(r):
+        return pltpu.make_async_remote_copy(
+            src_ref=kv_buf.at[part, rows_of(r), :],
+            dst_ref=kv_buf.at[part, rows_of(r), :],
+            send_sem=ex_send.at[r - 1],
+            recv_sem=ex_recv.at[r - 1],
+            device_id={"head": partner},
+            device_id_type=MESH,
+        )
+
+    def held(r):
+        return kv_buf.at[part, rows_of(r), :]
+
+    def forward(r):
+        @pl.when(me >= r)
+        def _():
+            hop(r, held(r)).wait_recv()
+            exchange(r).start()
+            if r < seen:
+                @pl.when(me < devices - 1)
+                def _():
+                    hop(r + 1, held(r)).start()
 
     def state_copy(h):
         return pltpu.make_async_remote_copy(
@@ -115,11 +143,12 @@
             device_id_type=MESH,
         )
 
-    for r in range(1, seen + 1):
-        @pl.when(me + r < devices)
-        def _():
-            for copy in kv_copies(r):
-                copy.start()
+    @pl.when(me < devices - 1)
+    def _():
+        for which, source in enumerate((ka_ref, va_ref)):
+            @pl.when(part == which)
+            def _():
+                hop(1, source.at[:, columns]).start()
 
     row = lax.broadcasted_iota(jnp.int32, (length, length), 0)
     col = lax.broadcasted_iota(jnp.int32, (length, length), 1)
@@ -215,8 +244,12 @@
                     state_copy(h).start()
 
     per_group = 4
+    ahead = 0
     for first in range(0, heads, per_group):
         state_part(list(range(first, min(first + per_group, heads))))
+        if ahead < seen:
+            ahead += 1
+            forward(ahead)
 
     def relay():
         for h in range(heads):
@@ -237,8 +270,8 @@
         relay()
 
     own = pl.ds(seen * length, length)
-    keys_buf[own, :] = ka_ref[:, columns]
-    vals_buf[own, :] = va_ref[:, columns]
+    kv_buf[0, own, :] = ka_ref[:, columns]
+    kv_buf[1, own, :] = va_ref[:, columns]
     for h in range(heads):
         made = dot(score_buf[h], solved_buf[h])
         local_buf[h] = made[:, :DV]
@@ -250,17 +283,16 @@
         def _():
             relay()
 
+    for r in range(ahead + 1, seen + 1):
+        forward(r)
     for r in range(1, seen + 1):
-        @pl.when(me - r >= 0)
-        def _():
-            for copy in kv_copies(r):
-                copy.wait_recv()
-
-        @pl.when(me - r < 0)
-        def _():
-            rows = pl.ds((seen - r) * length, length)
-            keys_buf[rows, :] = jnp.zeros((length, HD_A), BF)
-            vals_buf[rows, :] = jnp.zeros((length, HD_A), BF)
+        @pl.when(me >= r)
+        def _():
+            exchange(r).wait_recv()
+
+        @pl.when(me < r)
+        def _():
+            kv_buf[:, rows_of(r), :] = jnp.zeros((2, length, HD_A), BF)
 
     span = (seen + 1) * length
     window = (devices // 2 + 1) * length
@@ -271,12 +303,12 @@
     factor = HD_A ** (-0.5)
     for a in range(attn_heads):
         at = slice(a * HD_A, (a + 1) * HD_A)
-        raw = dot_t(qa_ref[:, at], keys_buf[...]) * factor
+        raw = dot_t(qa_ref[:, at], kv_buf[0]) * factor
         masked = jnp.where(visible, raw, NEG)
         peak = jnp.max(masked, axis=-1, keepdims=True)
         weights = jnp.exp(masked - peak)
         total = jnp.sum(weights, axis=-1, keepdims=True)
-        mixed = jnp.dot(weights.astype(BF), vals_buf[...], preferred_element_type=F32)
+        mixed = jnp.dot(weights.astype(BF), kv_buf[1], preferred_element_type=F32)
         gated = mixed / total * jax.nn.sigmoid(ga_ref[:, at].astype(F32))
         attn_ref[:, at] = gated.astype(BF)
 
@@ -293,11 +325,18 @@
         gate = z_ref[:, at].astype(F32)
         gdn_ref[:, at] = (mixed * spread * gain * jax.nn.silu(gate)).astype(BF)
 
+    @pl.when(me < devices - 1)
+    def _():
+        hop(1, held(1)).wait_send()
+
     for r in range(1, seen + 1):
-        @pl.when(me + r < devices)
-        def _():
-            for copy in kv_copies(r):
-                copy.wait_send()
+        @pl.when(me >= r)
+        def _():
+            exchange(r).wait_send()
+            if r < seen:
+                @pl.when(me < devices - 1)
+                def _():
+                    hop(r + 1, held(r)).wait_send()
 
     if devices > 1:
         @pl.when(me < devices - 1)
@@ -335,8 +374,7 @@
         in_specs=[whole] * 12,
         out_specs=(whole, whole),
         scratch_shapes=[
-            pltpu.VMEM((span, HD_A), BF),
-            pltpu.VMEM((span, HD_A), BF),
+            pltpu.VMEM((2, span, HD_A), BF),
             pltpu.VMEM((heads, DK, DV), BF),
             pltpu.VMEM((heads, DK, DV), BF),
             pltpu.VMEM((heads, length, DV), F32),
@@ -346,8 +384,10 @@
             pltpu.VMEM((q_gdn.shape[1] // DK, length, DK), BF),
             pltpu.VMEM((heads, length, length), BF),
             pltpu.VMEM((heads, length, DV + DK), BF),
-            pltpu.SemaphoreType.DMA((seen, 2)),
-            pltpu.SemaphoreType.DMA((seen, 2)),
+            pltpu.SemaphoreType.DMA((seen,)),
+            pltpu.SemaphoreType.DMA((seen,)),
+            pltpu.SemaphoreType.DMA((seen,)),
+            pltpu.SemaphoreType.DMA((seen,)),
             pltpu.SemaphoreType.DMA((heads,)),
             pltpu.SemaphoreType.DMA((heads,)),
         ],

time: 30.2 us -> 21.9 us (0.73)
  Pallas kernels: 27 us -> 18.7 us
    pallas_call x1, Pallas kernels: 27 us -> 18.7 us  [shards(): pl.pallas_call(functools.partial(kernel, devices, seen), out_shape=(jax.S...]
where the time goes in v3:
time: 21.9 us; the launch traced here: 21.8 us
  Pallas kernels  18.7 us (85%)
  local copies, waits for them, and re-layouts  2.42 us (11%)
  between operations  0.65 us (3%)
    pallas_call x1, Pallas kernels, shards(): pl.pallas_call(functools.partial(kernel, devices, seen), out_shape=(jax.S...  18.7 us
    unnamed x4, local copies, waits for them, and re-layouts  2.42 us

profile of v3, /device:TPU:26, one launch (start us, length us, event | category | flops | bytes accessed | tf_op | source)
XLA Modules:
  0.0 21.8 jit_solution(14548379974776110437)
XLA Ops:
  0.6 18.7 %shard_map.131 = (bf16[128,1024]{1,0:T(8,128)(2,1)}, bf16[128,1024]{1,0:T(8,128)(2,1)}) custom-call(s32[1,128]{1,0:T(1,128)} %bitcast.2, bf16[128,512]{1,0:T(8,128)(2,1)} %q_ref.1, bf16[128,512]{1,0:T(8,128)(2,1)} %k_ref.1, bf16[128,1024]{1,0:T(8,128)(2,1)} %v_ref.1, bf16[128,1024]{1,0:T(8,128)(2,1)} %z_ref.1, f32[8,128]{1,0:T(8,128)} %beta_ref.1, ...), custom_call_target="tpu_custom_call" | custom-call | tf_op jit(solution)/shard_map/pallas_call | solution.py:368
  19.4 0.0 copy-start
  19.4 1.7 %copy.16 = bf16[128,1024]{1,0:T(8,128)(2,1)} copy(bf16[128,1024]{1,0:T(8,128)(2,1)} %get-tuple-element.4) | data formatting | bytes 524288
  21.1 0.0 copy-done
  21.1 0.7 %copy.17 = bf16[128,1024]{1,0:T(8,128)(2,1)} copy(bf16[128,1024]{1,0:T(8,128)(2,1)S(1)} %copy-done) | data formatting | bytes 524288
Async XLA Ops:
  19.4 1.7 %copy-start = (bf16[128,1024]{1,0:T(8,128)(2,1)S(1)}, bf16[128,1024]{1,0:T(8,128)(2,1)}, u32[]{:S(2)}) copy-start(bf16[128,1024]{1,0:T(8,128)(2,1)} %get-tuple-element.5) | copy-start | bytes 786436

commit v4 on v3

--- a/solution.py
+++ b/solution.py
@@ -60,8 +60,9 @@
     reach_buf,
     map_buf,
     add_buf,
-    qn_buf,
-    score_buf,
+    kn_buf,
+    knt_buf,
+    decay_buf,
     solved_buf,
     kv_send,
     kv_recv,
@@ -195,44 +196,54 @@
     def unit_rows(values):
         return values * lax.rsqrt(square_sum(values) + 1e-06)
 
-    def state_part(group):
-        kn, knt, gram, cross = {}, {}, {}, {}
-        for g in sorted({h // repeat for h in group}):
-            at = slice(g * DK, (g + 1) * DK)
-            qn = unit_rows(q_ref[:, at].astype(F32)).astype(BF)
-            kn[g] = unit_rows(k_ref[:, at].astype(F32)).astype(BF)
-            qn_buf[g] = qn
-            knt[g] = kn[g].T
-            both = dot(jnp.concatenate([kn[g], qn], axis=0), knt[g])
-            gram[g], cross[g] = both[:length], both[length:]
-        inverse = {}
+    gram, knt, lower = {}, {}, {}
+
+    def key_part(g):
+        kn = unit_rows(k_ref[:, g * DK : (g + 1) * DK].astype(F32)).astype(BF)
+        knt[g] = kn.T
+        kn_buf[g] = kn
+        knt_buf[g] = knt[g]
+        gram[g] = dot(kn, knt[g])
+
+    def gate_part(h):
+        spread = jnp.where(same, column(0, h) - run[h : h + 1, :], 0.0)
+        decay = jnp.where(same, jnp.exp(spread), 0.0)
+        decay_buf[h] = decay
+        lower[h] = jnp.where(strict, column(1, h) * decay * gram[h // repeat], 0.0)
+
+    def preparations(group):
+        todo = []
         for h in group:
-            g = h // repeat
-            spread = jnp.where(same, column(0, h) - run[h : h + 1, :], 0.0)
-            decay = jnp.where(same, jnp.exp(spread), 0.0)
-            lower = jnp.where(strict, column(1, h) * decay * gram[g], 0.0)
-            score_buf[h] = (cross[g] * decay).astype(BF)
-            inverse[h] = eye + lower
+            if h // repeat not in gram:
+                gram[h // repeat] = None
+                todo.append(functools.partial(key_part, h // repeat))
+            todo.append(functools.partial(gate_part, h))
+        return todo
+
+    def state_part(group, beside):
+        beside = list(beside)
+        inverse = {h: eye + lower[h] for h in group}
         for level in range(levels):
             mask = (differ >> level) == 1
             for h in group:
                 whole = inverse[h]
                 part = jnp.where(mask, whole, 0.0)
                 inverse[h] = jnp.where(mask, 0.0, whole) - dot(part, whole)
-        solved = {}
+            if beside:
+                beside.pop(0)()
+        for task in beside:
+            task()
         for h in group:
             g = h // repeat
             values = v_ref[:, h * DV : (h + 1) * DV].astype(F32)
             b = column(1, h)
             right = jnp.concatenate(
-                [b * values, (b * column(2, h)) * kn[g].astype(F32)], axis=1
+                [b * values, (b * column(2, h)) * kn_buf[g].astype(F32)], axis=1
             )
-            solved[h] = dot(inverse[h], right).astype(BF)
-            solved_buf[h] = solved[h]
-        for h in group:
-            g = h // repeat
-            tail_keys = (knt[g].astype(F32) * tail[h : h + 1, :]).astype(BF)
-            made = dot(tail_keys, solved[h])
+            solved = dot(inverse[h], right).astype(BF)
+            solved_buf[h] = solved
+            tail_keys = (knt_buf[g].astype(F32) * tail[h : h + 1, :]).astype(BF)
+            made = dot(tail_keys, solved)
             map_buf[h] = (entry_last[h : h + 1, :] * eye - made[:, DV:]).astype(BF)
             add_buf[h] = made[:, :DV]
             state_out[h] = made[:, :DV].astype(BF)
@@ -244,9 +255,14 @@
                     state_copy(h).start()
 
     per_group = 4
+    groups = [
+        list(range(first, min(first + per_group, heads))) for first in range(0, heads, per_group)
+    ]
+    for task in preparations(groups[0]):
+        task()
     ahead = 0
-    for first in range(0, heads, per_group):
-        state_part(list(range(first, min(first + per_group, heads))))
+    for at, group in enumerate(groups):
+        state_part(group, preparations(groups[at + 1]) if at + 1 < len(groups) else ())
         if ahead < seen:
             ahead += 1
             forward(ahead)
@@ -272,11 +288,13 @@
     own = pl.ds(seen * length, length)
     kv_buf[0, own, :] = ka_ref[:, columns]
     kv_buf[1, own, :] = va_ref[:, columns]
-    for h in range(heads):
-        made = dot(score_buf[h], solved_buf[h])
-        local_buf[h] = made[:, :DV]
-        through = column(2, h) * qn_buf[h // repeat].astype(F32)
-        reach_buf[h] = (through - made[:, DV:]).astype(BF)
+    for g in range(key_heads):
+        qn = unit_rows(q_ref[:, g * DK : (g + 1) * DK].astype(F32)).astype(BF)
+        cross = dot(qn, knt_buf[g])
+        for h in range(g * repeat, (g + 1) * repeat):
+            made = dot(cross * decay_buf[h], solved_buf[h])
+            local_buf[h] = made[:, :DV]
+            reach_buf[h] = (column(2, h) * qn.astype(F32) - made[:, DV:]).astype(BF)
 
     if devices > 2:
         @pl.when(me == 2)
@@ -368,8 +386,8 @@
     return pl.pallas_call(
         functools.partial(kernel, devices, seen),
         out_shape=(
-            jax.ShapeDtypeStruct(v_gdn.shape, BF),
-            jax.ShapeDtypeStruct(q_attn.shape, BF),
+            pltpu.VMEM(v_gdn.shape, BF),
+            pltpu.VMEM(q_attn.shape, BF),
         ),
         in_specs=[whole] * 12,
         out_specs=(whole, whole),
@@ -382,7 +400,8 @@
             pltpu.VMEM((heads, DK, DK), BF),
             pltpu.VMEM((heads, DK, DV), F32),
             pltpu.VMEM((q_gdn.shape[1] // DK, length, DK), BF),
-            pltpu.VMEM((heads, length, length), BF),
+            pltpu.VMEM((q_gdn.shape[1] // DK, DK, length), BF),
+            pltpu.VMEM((heads, length, length), F32),
             pltpu.VMEM((heads, length, DV + DK), BF),
             pltpu.SemaphoreType.DMA((seen,)),
             pltpu.SemaphoreType.DMA((seen,)),

time: 21.9 us -> 20.4 us (0.932)
  local copies, waits for them, and re-layouts: 2.42 us -> 1.41 us
  Pallas kernels: 18.7 us -> 18.2 us
    unnamed x4 -> x2, local copies, waits for them, and re-layouts: 2.42 us -> 1.41 us
    pallas_call x1, Pallas kernels: 18.7 us -> 18.2 us  [shards(): pl.pallas_call(functools.partial(kernel, devices, seen), out_shape=(pltpu...]
where the time goes in v4:
time: 20.4 us; the launch traced here: 20.3 us
  Pallas kernels  18.2 us (89%)
  local copies, waits for them, and re-layouts  1.41 us (7%)
  between operations  0.64 us (3%)
    pallas_call x1, Pallas kernels, shards(): pl.pallas_call(functools.partial(kernel, devices, seen), out_shape=(pltpu...  18.2 us
    unnamed x2, local copies, waits for them, and re-layouts  1.41 us

profile of v4, /device:TPU:26, one launch (start us, length us, event | category | flops | bytes accessed | tf_op | source)
XLA Modules:
  0.0 20.3 jit_solution(10523004332093564622)
XLA Ops:
  0.6 18.2 %shard_map.131 = (bf16[128,1024]{1,0:T(8,128)(2,1)S(1)}, bf16[128,1024]{1,0:T(8,128)(2,1)S(1)}) custom-call(s32[1,128]{1,0:T(1,128)} %bitcast.2, bf16[128,512]{1,0:T(8,128)(2,1)} %q_ref.1, bf16[128,512]{1,0:T(8,128)(2,1)} %k_ref.1, bf16[128,1024]{1,0:T(8,128)(2,1)} %v_ref.1, bf16[128,1024]{1,0:T(8,128)(2,1)} %z_ref.1, f32[8,128]{1,0:T(8,128)} %beta_ref.1, ...), custom_call_target="tpu_custom_call" | custom-call | tf_op jit(solution)/shard_map/pallas_call | solution.py:386
  18.8 0.7 %copy.16 = bf16[128,1024]{1,0:T(8,128)(2,1)} copy(bf16[128,1024]{1,0:T(8,128)(2,1)S(1)} %get-tuple-element.2) | data formatting | bytes 524288
  19.6 0.7 %copy.17 = bf16[128,1024]{1,0:T(8,128)(2,1)} copy(bf16[128,1024]{1,0:T(8,128)(2,1)S(1)} %get-tuple-element.3) | data formatting | bytes 524288

commit v5 on v4

--- a/solution.py
+++ b/solution.py
@@ -254,7 +254,7 @@
                 for h in group:
                     state_copy(h).start()
 
-    per_group = 4
+    per_group = 2
     groups = [
         list(range(first, min(first + per_group, heads))) for first in range(0, heads, per_group)
     ]
@@ -263,12 +263,12 @@
     ahead = 0
     for at, group in enumerate(groups):
         state_part(group, preparations(groups[at + 1]) if at + 1 < len(groups) else ())
-        if ahead < seen:
+        if at % 2 == 1 and ahead < seen:
             ahead += 1
             forward(ahead)
 
-    def relay():
-        for h in range(heads):
+    def relay(chosen):
+        for h in chosen:
             state_copy(h).wait_recv()
 
             @pl.when(me < devices - 1)
@@ -283,7 +283,7 @@
 
     @pl.when(me == 1)
     def _():
-        relay()
+        relay(range(heads))
 
     own = pl.ds(seen * length, length)
     kv_buf[0, own, :] = ka_ref[:, columns]
@@ -299,7 +299,7 @@
     if devices > 2:
         @pl.when(me == 2)
         def _():
-            relay()
+            relay(range(heads))
 
     for r in range(ahead + 1, seen + 1):
         forward(r)
@@ -330,18 +330,20 @@
         gated = mixed / total * jax.nn.sigmoid(ga_ref[:, at].astype(F32))
         attn_ref[:, at] = gated.astype(BF)
 
-    if devices > 3:
-        @pl.when(me >= 3)
-        def _():
-            relay()
-
     gain = norm_ref[...]
-    for h in range(heads):
-        at = slice(h * DV, (h + 1) * DV)
-        mixed = local_buf[h] + dot(reach_buf[h], state_in[h])
-        spread = lax.rsqrt(square_sum(mixed) * (1.0 / DV) + 1e-06)
-        gate = z_ref[:, at].astype(F32)
-        gdn_ref[:, at] = (mixed * spread * gain * jax.nn.silu(gate)).astype(BF)
+    for first in range(0, heads, per_group):
+        chosen = range(first, min(first + per_group, heads))
+        if devices > 3:
+            @pl.when(me >= 3)
+            def _():
+                relay(chosen)
+
+        for h in chosen:
+            at = slice(h * DV, (h + 1) * DV)
+            mixed = local_buf[h] + dot(reach_buf[h], state_in[h])
+            spread = lax.rsqrt(square_sum(mixed) * (1.0 / DV) + 1e-06)
+            gate = z_ref[:, at].astype(F32)
+            gdn_ref[:, at] = (mixed * spread * gain * jax.nn.silu(gate)).astype(BF)
 
     @pl.when(me < devices - 1)
     def _():
@@ -361,6 +363,17 @@
         def _():
             for h in range(heads):
                 state_copy(h).wait_send()
+
+
+def store(first_ref, second_ref, first_out, second_out, sems):
+    copies = [
+        pltpu.make_async_copy(first_ref, first_out, sems.at[0]),
+        pltpu.make_async_copy(second_ref, second_out, sems.at[1]),
+    ]
+    for copy in copies:
+        copy.start()
+    for copy in copies:
+        copy.wait()
 
 
 def shards(
@@ -383,7 +396,7 @@
     seen = min(devices // 2 + 1, devices - 1)
     span = (seen + 1) * length
     whole = pl.BlockSpec(memory_space=pltpu.VMEM)
-    return pl.pallas_call(
+    mixed = pl.pallas_call(
         functools.partial(kernel, devices, seen),
         out_shape=(
             pltpu.VMEM(v_gdn.shape, BF),
@@ -426,6 +439,18 @@
         gate_attn,
     )
 
+    anywhere = pl.BlockSpec(memory_space=pl.ANY)
+    return pl.pallas_call(
+        store,
+        out_shape=(
+            jax.ShapeDtypeStruct(v_gdn.shape, BF),
+            jax.ShapeDtypeStruct(q_attn.shape, BF),
+        ),
+        in_specs=[whole] * 2,
+        out_specs=(anywhere, anywhere),
+        scratch_shapes=[pltpu.SemaphoreType.DMA((2,))],
+    )(*[pltpu.with_memory_space_constraint(array, pltpu.VMEM) for array in mixed])
+
 
 def solution(mesh):
     return jax.shard_map(

time: 20.4 us -> 20.5 us (level)
  local copies, waits for them, and re-layouts: 1.41 us -> 0 us
  Pallas kernels: 18.2 us -> 19.6 us
    unnamed x2 -> x0, local copies, waits for them, and re-layouts: 1.41 us -> none
    pallas_call x0 -> x1, Pallas kernels: none -> 0.81 us  [shards(): pl.pallas_call(store, out_shape=(jax.ShapeDtypeStruct(v_gdn.shape, BF), j...]
    pallas_call x1, Pallas kernels: 18.2 us -> 18.8 us  [shards(): pl.pallas_call(functools.partial(kernel, devices, seen), out_shape=(pltpu...]
where the time goes in v5:
time: 20.5 us; the launch traced here: 20.3 us
  Pallas kernels  19.6 us (96%)
  between operations  0.64 us (3%)
    pallas_call x1, Pallas kernels, shards(): pl.pallas_call(functools.partial(kernel, devices, seen), out_shape=(pltpu...  18.8 us
    pallas_call x1, Pallas kernels, shards(): pl.pallas_call(store, out_shape=(jax.ShapeDtypeStruct(v_gdn.shape, BF), j...  0.81 us

profile of v5, /device:TPU:26, one launch (start us, length us, event | category | flops | bytes accessed | tf_op | source)
XLA Modules:
  0.0 20.3 jit_solution(4967066250008258855)
XLA Ops:
  0.6 18.8 %shard_map.131 = (bf16[128,1024]{1,0:T(8,128)(2,1)S(1)}, bf16[128,1024]{1,0:T(8,128)(2,1)S(1)}) custom-call(s32[1,128]{1,0:T(1,128)} %bitcast.2, bf16[128,512]{1,0:T(8,128)(2,1)} %q_ref.1, bf16[128,512]{1,0:T(8,128)(2,1)} %k_ref.1, bf16[128,1024]{1,0:T(8,128)(2,1)} %v_ref.1, bf16[128,1024]{1,0:T(8,128)(2,1)} %z_ref.1, f32[8,128]{1,0:T(8,128)} %beta_ref.1, ...), custom_call_target="tpu_custom_call" | custom-call | tf_op jit(solution)/shard_map/pallas_call | solution.py:399
  19.5 0.8 %shard_map.132 = (bf16[128,1024]{1,0:T(8,128)(2,1)}, bf16[128,1024]{1,0:T(8,128)(2,1)}) custom-call(bf16[128,1024]{1,0:T(8,128)(2,1)S(1)} %get-tuple-element.4.first_ref, bf16[128,1024]{1,0:T(8,128)(2,1)S(1)} %get-tuple-element.5.second_ref), custom_call_target="tpu_custom_call" | custom-call | tf_op jit(solution)/shard_map/pallas_call | solution.py:443

commit v6 on v5

--- a/solution.py
+++ b/solution.py
@@ -254,7 +254,7 @@
                 for h in group:
                     state_copy(h).start()
 
-    per_group = 2
+    per_group = 4
     groups = [
         list(range(first, min(first + per_group, heads))) for first in range(0, heads, per_group)
     ]
@@ -263,7 +263,7 @@
     ahead = 0
     for at, group in enumerate(groups):
         state_part(group, preparations(groups[at + 1]) if at + 1 < len(groups) else ())
-        if at % 2 == 1 and ahead < seen:
+        if ahead < seen:
             ahead += 1
             forward(ahead)
 
@@ -331,8 +331,9 @@
         attn_ref[:, at] = gated.astype(BF)
 
     gain = norm_ref[...]
-    for first in range(0, heads, per_group):
-        chosen = range(first, min(first + per_group, heads))
+    pair = 2
+    for first in range(0, heads, pair):
+        chosen = range(first, min(first + pair, heads))
         if devices > 3:
             @pl.when(me >= 3)
             def _():

time: 20.5 us -> 19.3 us (0.941)
  Pallas kernels: 19.6 us -> 18.4 us
    pallas_call x1, Pallas kernels: 18.8 us -> 17.6 us  [shards(): pl.pallas_call(functools.partial(kernel, devices, seen), out_shape=(pltpu...]
where the time goes in v6:
time: 19.3 us; the launch traced here: 19.1 us
  Pallas kernels  18.4 us (95%)
  between operations  0.64 us (3%)
    pallas_call x1, Pallas kernels, shards(): pl.pallas_call(functools.partial(kernel, devices, seen), out_shape=(pltpu...  17.6 us
    pallas_call x1, Pallas kernels, shards(): pl.pallas_call(store, out_shape=(jax.ShapeDtypeStruct(v_gdn.shape, BF), j...  0.81 us

profile of v6, /device:TPU:26, one launch (start us, length us, event | category | flops | bytes accessed | tf_op | source)
XLA Modules:
  0.0 19.1 jit_solution(9941286643331640483)
XLA Ops:
  0.6 17.6 %shard_map.131 = (bf16[128,1024]{1,0:T(8,128)(2,1)S(1)}, bf16[128,1024]{1,0:T(8,128)(2,1)S(1)}) custom-call(s32[1,128]{1,0:T(1,128)} %bitcast.2, bf16[128,512]{1,0:T(8,128)(2,1)} %q_ref.1, bf16[128,512]{1,0:T(8,128)(2,1)} %k_ref.1, bf16[128,1024]{1,0:T(8,128)(2,1)} %v_ref.1, bf16[128,1024]{1,0:T(8,128)(2,1)} %z_ref.1, f32[8,128]{1,0:T(8,128)} %beta_ref.1, ...), custom_call_target="tpu_custom_call" | custom-call | tf_op jit(solution)/shard_map/pallas_call | solution.py:400
  18.3 0.8 %shard_map.132 = (bf16[128,1024]{1,0:T(8,128)(2,1)}, bf16[128,1024]{1,0:T(8,128)(2,1)}) custom-call(bf16[128,1024]{1,0:T(8,128)(2,1)S(1)} %get-tuple-element.4.first_ref, bf16[128,1024]{1,0:T(8,128)(2,1)S(1)} %get-tuple-element.5.second_ref), custom_call_target="tpu_custom_call" | custom-call | tf_op jit(solution)/shard_map/pallas_call | solution.py:444
